TPU v7x, 128 devices: a whole 4x4x4 slice. The times are simulated.
128 devices in a mesh: row: 8 (over z, core), col: 16 (over x, y).
Axes of the slice: x: 4, y: 4, z: 4, core: 2. Of those that a mesh axis runs over, the one named last changes fastest.
Arguments:
- a_blocks: float32 [1024, 8, 256, 256], P(('row', 'col')), may hold values from -0.09375 to 0.09375
- a_live: int32 [1024, 8], P(('row', 'col')), may hold values from 0 to 1, as said below
- p_blocks: float32 [1024, 256, 2, 128], P(('row', 'col')), may hold values from -0.1875 to 0.1875
- p_cols: int32 [1024, 2], P(('row', 'col')), may hold values from 0 to 127, as said below
- ghost_list: int32 [1024, 7], P(('row', 'col')), may hold values from 0 to 7, as said below
- policy: int32 [1024], P(('row', 'col')), may hold values from 0 to 15
- rates: float32 [16, 256], replicated, may hold values from 0.1 to 1
- rhs: float32 [16384, 256], P(('row', 'col')), may hold values from -6 to 6
- guess: float32 [16384, 256], P(('row', 'col')), may hold values from -6 to 6
Outputs:
- coarse: float32 [16384, 8, 16, 128], P('row', None, 'col')
- smoothed: float32 [16384, 256], P(('row', 'col'))
Inputs may be any that keep to these rules, and one draw needn't show every extreme that they name: a_live[i, 0] is 1 for every i. On each device and for each k, the entries ghost_list[d * 8 + s, k] over s = 0 .. 7 are a permutation of 0 .. 7. p_cols[j, m] modulo the number of col devices equals (col index of the device holding block row j + m * 8) modulo that number. The quotient by that number names a mesh row: among the 16 entries of one device at most 2 name the same mesh row, and the device's own mesh row is named exactly 2 times, by at least one entry of each m.
All inputs are finite; a program needn't handle non-finite values.
Results may differ from a plain program's by a relative error of at most 0.0003.
Values sent between devices are 32-bit elements; how exact they have to be, the bound alone decides.
No kernel may reach another device: no remote copies, remote signals or barrier semaphores. Data moves between devices by JAX's collectives and lax.ppermute only.
A program may use at most 192 MiB of HBM per device.

v0:
```python
import jax
import jax.numpy as jnp
from jax import lax
from jax.sharding import PartitionSpec as P

BS = 256
CB = 128
KA = 8
KP = 2
NPOL = 16
damping = 0.7


def from_behind(value, axis, steps):
    count = lax.axis_size(axis)
    pairs = [(source, (source + steps) % count) for source in range(count)]
    return lax.ppermute(value, axis, pairs)


def on_device(a_blocks, a_live, p_blocks, p_cols, ghost_list, policy, rates, rhs, guess):
    highest = lax.Precision.HIGHEST
    row_count = lax.axis_size("row")
    col_count = lax.axis_size("col")
    dev_count = row_count * col_count
    row_here = lax.axis_index("row")
    col_here = lax.axis_index("col")
    local_rows = a_blocks.shape[0]
    own_p = p_blocks.reshape(local_rows, BS, KP * CB)
    send_p = []
    send_c = []
    for offset in range(1, KA):
        picks = ghost_list[:, offset - 1]
        send_p.append(own_p[picks])
        send_c.append(p_cols[picks].astype(jnp.float32))
    incoming_p = [own_p]
    incoming_c = [p_cols]
    for offset in range(1, KA):
        moved_p, moved_c = from_behind((send_p[offset - 1], send_c[offset - 1]), "col", offset)
        incoming_p.append(moved_p)
        incoming_c.append(moved_c.astype(jnp.int32))
    ghost_p = jnp.stack(incoming_p, axis=1)
    ghost_c = jnp.stack(incoming_c, axis=1)
    live = a_live.astype(jnp.float32)
    selector = (policy[:, None] == jnp.arange(NPOL, dtype=jnp.int32)[None, :]).astype(jnp.float32)
    rate_rows = jnp.dot(selector, rates, precision=highest)
    product = jnp.einsum("skab,skbn->skan", a_blocks, ghost_p, precision=highest)
    product = product * live[:, :, None, None]
    product = product.at[:, 0].add(rate_rows[:, :, None] * own_p)
    partial_value = jnp.einsum("sam,skan->skmn", own_p, product, precision=highest)
    partial_value = (
        partial_value.reshape(local_rows, KA, KP, CB, KP, CB)
        .transpose(0, 1, 2, 4, 3, 5)
        .reshape(-1, CB, CB)
    )
    first = jnp.broadcast_to(p_cols[:, None, :, None], (local_rows, KA, KP, KP)).reshape(-1)
    second = jnp.broadcast_to(ghost_c[:, :, None, :], (local_rows, KA, KP, KP)).reshape(-1)
    alive = jnp.broadcast_to(a_live[:, :, None, None] > 0, (local_rows, KA, KP, KP)).reshape(-1)
    owner = first // col_count * col_count + second % col_count
    spot = first % col_count * row_count + second // col_count
    order = jnp.arange(owner.shape[0], dtype=jnp.int32)
    earlier = (
        (owner[None, :] == owner[:, None]) & alive[None, :] & (order[None, :] < order[:, None])
    )
    rank = jnp.sum(earlier.astype(jnp.int32), axis=1)
    row_cap = max(2, -(-(local_rows * KP) // row_count))
    slot_cap = row_cap * max(1, KA * KP // col_count)
    slot = jnp.where(alive, owner * slot_cap + rank, dev_count * slot_cap)
    sent_blocks = jax.ops.segment_sum(partial_value, slot, num_segments=dev_count * slot_cap + 1)[
        :-1
    ]
    sent_spots = jax.ops.segment_sum(
        (spot + 1).astype(jnp.float32), slot, num_segments=dev_count * slot_cap + 1
    )[:-1]
    got_blocks, got_spots = (
        lax.all_to_all(
            sent_blocks.reshape(dev_count, slot_cap, CB, CB),
            ("row", "col"),
            split_axis=0,
            concat_axis=0,
            tiled=True,
        ),
        lax.all_to_all(
            sent_spots.reshape(dev_count, slot_cap),
            ("row", "col"),
            split_axis=0,
            concat_axis=0,
            tiled=True,
        ),
    )
    places = got_spots.reshape(-1).astype(jnp.int32) - 1
    places = jnp.where(places < 0, dev_count, places)
    summed = jax.ops.segment_sum(
        got_blocks.reshape(-1, CB, CB), places, num_segments=dev_count + 1
    )[:-1]
    coarse = (
        summed.reshape(col_count, row_count, CB, CB)
        .transpose(0, 2, 1, 3)
        .reshape(col_count * CB, row_count, 1, CB)
    )
    matrix = coarse.reshape(col_count * CB, row_count * CB)
    own_block = lax.dynamic_slice(matrix, (col_here * CB, row_here * CB), (CB, CB))
    floor_diag = jnp.maximum(jnp.abs(jnp.diagonal(own_block)), 1.0)
    current = guess
    for sweep in range(2):
        gathered = lax.all_gather(current, "row", axis=0, tiled=True)
        applied = lax.psum_scatter(
            jnp.dot(matrix, gathered, precision=highest), "col", scatter_dimension=0, tiled=True
        )
        current = current + damping * (rhs - applied) / floor_diag[:, None]
    return (coarse, current)


def solution(mesh):
    return jax.shard_map(
        on_device,
        mesh=mesh,
        in_specs=(
            P(("row", "col"), None, None, None),
            P(("row", "col"), None),
            P(("row", "col"), None, None, None),
            P(("row", "col"), None),
            P(("row", "col"), None),
            P(("row", "col")),
            P(),
            P(("row", "col"), None),
            P(("row", "col"), None),
        ),
        out_specs=(P("row", None, "col", None), P(("row", "col"), None)),
        check_vma=False,
    )
```

profile of v0, /device:TPU:0, one launch (start us, length us, event | category | flops | bytes accessed | tf_op | source)
XLA Modules:
  0.0 1113.7 jit_solution(12962005515692555085)
XLA Ops:
  9.8 3.4 collective-permute-start.1
  15.0 3.6 collective-permute-start.2
  34.1 4.1 copy.128
  50.5 4.1 reshape.490
  56.4 3.1 copy.132
  75.2 47.6 %collective-permute-start.9 = (f32[8,256,256]{1,2,0:T(8,128)}, f32[8,256,256]{1,2,0:T(8,128)}, u32[]{:S(2)}, u32[]{:S(2)}) collective-permute-start(f32[8,256,256]{1,2,0:T(8,128)} %copy.131), channel_id=1, source_target_pairs={{0,3},{1,4},{2,5},{3,6},{4,7},{5,8},{6,9},{7,10},{8,11},{9,12},{10... | collective-permute-start | bytes 6291464 | tf_op jit(solution)/shard_map/ppermute | solution.py:17
  123.9 44.1 %collective-permute-done.6 = f32[8,2]{1,0:T(8,128)S(1)} collective-permute-done((f32[8,2]{1,0:T(8,128)S(1)}, f32[8,2]{1,0:T(8,128)S(1)}, u32[]{:S(2)}, u32[]{:S(2)}) %collective-permute-start.6) | collective-permute-done | bytes 96 | tf_op jit(solution)/shard_map/ppermute | solution.py:17
  168.4 47.3 %collective-permute-start.12 = (f32[8,256,256]{1,2,0:T(8,128)}, f32[8,256,256]{1,2,0:T(8,128)}, u32[]{:S(2)}, u32[]{:S(2)}) collective-permute-start(f32[8,256,256]{1,2,0:T(8,128)} %copy.134), channel_id=1, source_target_pairs={{0,6},{1,7},{2,8},{3,9},{4,10},{5,11},{6,12},{7,13},{8,14},{9,15},... | collective-permute-start | bytes 6291464 | tf_op jit(solution)/shard_map/ppermute | solution.py:17
  216.0 6.1 collective-permute-start.13
  225.3 7.6 all-to-all-start
  244.9 16.2 %collective-permute-done.11 = f32[8,256,256]{1,2,0:T(8,128)} collective-permute-done((f32[8,256,256]{1,2,0:T(8,128)}, f32[8,256,256]{1,2,0:T(8,128)}, u32[]{:S(2)}, u32[]{:S(2)}) %collective-permute-start.11) | collective-permute-done | bytes 2097184 | tf_op jit(solution)/shard_map/ppermute | solution.py:17
  264.1 88.1 %collective-permute-done.12 = f32[8,256,256]{1,2,0:T(8,128)} collective-permute-done((f32[8,256,256]{1,2,0:T(8,128)}, f32[8,256,256]{1,2,0:T(8,128)}, u32[]{:S(2)}, u32[]{:S(2)}) %collective-permute-start.12) | collective-permute-done | bytes 2097184 | tf_op jit(solution)/shard_map/ppermute | solution.py:17
  358.2 43.2 %multiply_bitcast_fusion = f32[8,8,256,256]{2,3,1,0:T(8,128)} fusion(f32[8,8,256,256]{2,3,1,0:T(8,128)} %bitcast_dynamic-update-slice_fusion, f32[8,8,256,256]{3,2,1,0:T(8,128)} %param.11, f32[8,8]{1,0:T(8,128)S(1)} %convert_element_type.80), kind=kOutput, calls=%fused_computation.18 | convolution fusion | flops 12889096192 | bytes 50331904 | tf_op jit(solution)/shard_map/skab,skbn->skan/dot_general | solution.py:46
  401.4 3.3 fusion
  404.7 21.4 %convolution_bitcast_fusion = f32[8,8,256,256]{2,3,1,0:T(8,128)} fusion(f32[8,8,256,256]{2,3,1,0:T(8,128)} %fusion, f32[8,256,256,1]{2,1,0,3:T(8,128)S(1)} %copy-done.3), kind=kOutput, calls=%fused_computation.19 | convolution fusion | flops 12884901888 | bytes 35651584 | tf_op jit(solution)/shard_map/sam,skan->skmn/dot_general | solution.py:49
  426.1 20.8 %reshape.342 = f32[8,8,2,128,2,128]{3,2,5,4,1,0:T(2,128)} reshape(f32[8,8,256,256]{2,3,1,0:T(8,128)} %convolution_bitcast_fusion) | data formatting | bytes 33554432 | tf_op jit(solution)/shard_map/reshape | solution.py:51
  446.9 25.0 %copy.136 = f32[8,8,2,128,2,128]{5,3,4,2,1,0:T(8,128)} copy(f32[8,8,2,128,2,128]{3,2,5,4,1,0:T(2,128)} %reshape.342) | data formatting | bytes 33554432 | tf_op jit(solution)/shard_map/reshape | solution.py:51
  471.9 7.9 broadcast_in_dim.27
  479.7 51.5 %scatter_fusion = f32[257,128,128]{2,1,0:T(8,128)} fusion(f32[257,128,128]{2,1,0:T(8,128)} %broadcast_in_dim.27, s32[256]{0:T(256)S(1)} %bitcast.83, f32[256,128,128]{2,1,0:T(8,128)} %bitcast.77), kind=kCustom, calls=%fused_computation.16 | custom fusion | flops 4194304 | bytes 50332672 | tf_op jit(solution)/shard_map/scatter-add | solution.py:68
  531.3 11.6 %slice.99 = f32[256,128,128]{2,1,0:T(8,128)} slice(f32[257,128,128]{2,1,0:T(8,128)} %scatter_fusion), slice={[0:256], [0:128], [0:128]} | slice | bytes 33554432 | tf_op jit(solution)/shard_map/slice | solution.py:68
  542.9 50.5 %all-to-all-start.1 = ((f32[128,2,128,128]{3,2,1,0:T(8,128)}), f32[128,2,128,128]{3,2,1,0:T(8,128)}, u32[]{:S(2)}, u32[]{:S(2)}) async-start(f32[128,2,128,128]{3,2,1,0:T(8,128)} %bitcast.76), calls=%async_computation.1 | async-start | bytes 33554432 | tf_op jit(solution)/shard_map/all_to_all | solution.py:75
  595.0 237.9 %all-to-all-done.1 = f32[128,2,128,128]{3,2,1,0:T(8,128)} async-done(((f32[128,2,128,128]{3,2,1,0:T(8,128)}), f32[128,2,128,128]{3,2,1,0:T(8,128)}, u32[]{:S(2)}, u32[]{:S(2)}) %all-to-all-start.1) | async-done | bytes 16777248 | tf_op jit(solution)/shard_map/all_to_all | solution.py:75
  832.9 4.3 broadcast_in_dim.20
  837.3 51.8 %scatter_fusion.1 = f32[129,128,128]{2,1,0:T(8,128)} fusion(f32[129,128,128]{2,1,0:T(8,128)} %broadcast_in_dim.20, s32[256]{0:T(256)S(1)} %bitcast.84, f32[256,128,128]{2,1,0:T(8,128)} %bitcast.26), kind=kCustom, calls=%fused_computation.17 | custom fusion | flops 4194304 | bytes 50332672 | tf_op jit(solution)/shard_map/scatter-add | solution.py:92
  889.1 4.0 slice.100
  893.0 9.9 copy.137
  903.0 11.6 %fusion.20 = f32[2048,256]{1,0:T(8,128)} fusion(f32[1024,256]{1,0:T(8,128)} %all-gather.3.cloned.1.call-done, f32[256,8,8,128]{3,2,1,0:T(8,128)} %bitcast.72), kind=kOutput, calls=%fused_computation.105 | convolution fusion | flops 6442450944 | bytes 11534336 | tf_op jit(solution)/shard_map/dot_general | solution.py:107
  914.7 5.5 copy.145
  921.5 72.0 %reduce-scatter.3.cloned.1.call-done = f32[128,256]{1,0:T(8,128)} async-done(((f32[2048,256]{1,0:T(8,128)}), f32[128,256]{1,0:T(8,128)}) %reduce-scatter.3.cloned.1.call-update) | async-done | bytes 131088 | tf_op jit(solution)/shard_map/reduce_scatter | solution.py:106
  995.2 23.5 %all-gather.5.cloned.1.call-done = f32[1024,256]{1,0:T(8,128)} async-done(((f32[128,256]{1,0:T(8,128)}), f32[1024,256]{1,0:T(8,128)}) %all-gather.5.cloned.1.call-update) | async-done | bytes 1048592 | tf_op jit(solution)/shard_map/all_gather | solution.py:105
  1018.7 11.5 %fusion.19 = f32[2048,256]{1,0:T(8,128)} fusion(f32[1024,256]{1,0:T(8,128)} %all-gather.5.cloned.1.call-done, f32[256,8,8,128]{3,2,1,0:T(8,128)} %bitcast.74), kind=kOutput, calls=%fused_computation.104 | convolution fusion | flops 6442450944 | bytes 11534336 | tf_op jit(solution)/shard_map/dot_general | solution.py:107
  1030.2 75.1 %reduce-scatter.5.cloned.1.call-done = f32[128,256]{1,0:T(8,128)} async-done(((f32[2048,256]{1,0:T(8,128)}), f32[128,256]{1,0:T(8,128)}) %reduce-scatter.5.cloned.1.call-update) | async-done | bytes 131088 | tf_op jit(solution)/shard_map/reduce_scatter | solution.py:106
  (146 shorter events, 82.0 us)
Async XLA Ops:
  7.2 25.8 %copy-start = (f32[16,256]{1,0:T(8,128)S(1)}, f32[16,256]{1,0:T(8,128)}, u32[]{:S(2)}) copy-start(f32[16,256]{1,0:T(8,128)} %param.17) | copy-start | bytes 49156
  9.8 59.1 %collective-permute-start.1 = (f32[8,2]{1,0:T(8,128)S(1)}, f32[8,2]{1,0:T(8,128)S(1)}, u32[]{:S(2)}, u32[]{:S(2)}) collective-permute-start(f32[8,2]{1,0:T(8,128)S(1)} %convert_element_type.65), channel_id=1, source_target_pairs={{0,2},{1,3},{2,4},{3,5},{4,6},{5,7},{6,8},{7,9},{8,10},{9,11},{10,... | collective-permute-start | bytes 200 | tf_op jit(solution)/shard_map/ppermute | solution.py:17
  13.7 56.4 %collective-permute-start = (f32[8,2]{1,0:T(8,128)S(1)}, f32[8,2]{1,0:T(8,128)S(1)}, u32[]{:S(2)}, u32[]{:S(2)}) collective-permute-start(f32[8,2]{1,0:T(8,128)S(1)} %convert_element_type.63), channel_id=1, source_target_pairs={{0,1},{1,2},{2,3},{3,4},{4,5},{5,6},{6,7},{7,8},{8,9},{9,10},{10,1... | collective-permute-start | bytes 200 | tf_op jit(solution)/shard_map/ppermute | solution.py:17
  15.0 57.9 %collective-permute-start.2 = (f32[8,2]{1,0:T(8,128)S(1)}, f32[8,2]{1,0:T(8,128)S(1)}, u32[]{:S(2)}, u32[]{:S(2)}) collective-permute-start(f32[8,2]{1,0:T(8,128)S(1)} %convert_element_type.67), channel_id=1, source_target_pairs={{0,3},{1,4},{2,5},{3,6},{4,7},{5,8},{6,9},{7,10},{8,11},{9,12},{10... | collective-permute-start | bytes 200 | tf_op jit(solution)/shard_map/ppermute | solution.py:17
  26.4 141.9 %collective-permute-start.8 = (f32[8,256,256]{1,2,0:T(8,128)}, f32[8,256,256]{1,2,0:T(8,128)}, u32[]{:S(2)}, u32[]{:S(2)}) collective-permute-start(f32[8,256,256]{1,2,0:T(8,128)} %copy.130), channel_id=1, source_target_pairs={{0,2},{1,3},{2,4},{3,5},{4,6},{5,7},{6,8},{7,9},{8,10},{9,11},{10,... | collective-permute-start | bytes 6291464 | tf_op jit(solution)/shard_map/ppermute | solution.py:17
  28.5 4.5 copy-start.10
  28.5 4.5 copy-start.9
  28.5 4.5 copy-start.11
  31.4 184.6 %collective-permute-start.7 = (f32[8,256,256]{1,2,0:T(8,128)}, f32[8,256,256]{1,2,0:T(8,128)}, u32[]{:S(2)}, u32[]{:S(2)}) collective-permute-start(f32[8,256,256]{1,2,0:T(8,128)} %copy.129), channel_id=1, source_target_pairs={{0,1},{1,2},{2,3},{3,4},{4,5},{5,6},{6,7},{7,8},{8,9},{9,10},{10,1... | collective-permute-start | bytes 6291464 | tf_op jit(solution)/shard_map/ppermute | solution.py:17
  50.5 4.1 copy-start.4
  56.4 3.1 copy-start.5
  61.4 3.0 copy-start.2
  68.8 6.4 collective-permute-start.3
  70.1 52.7 %collective-permute-start.4 = (f32[8,2]{1,0:T(8,128)S(1)}, f32[8,2]{1,0:T(8,128)S(1)}, u32[]{:S(2)}, u32[]{:S(2)}) collective-permute-start(f32[8,2]{1,0:T(8,128)S(1)} %convert_element_type.71), channel_id=1, source_target_pairs={{0,5},{1,6},{2,7},{3,8},{4,9},{5,10},{6,11},{7,12},{8,13},{9,14},{... | collective-permute-start | bytes 200 | tf_op jit(solution)/shard_map/ppermute | solution.py:17
  72.9 50.3 %collective-permute-start.5 = (f32[8,2]{1,0:T(8,128)S(1)}, f32[8,2]{1,0:T(8,128)S(1)}, u32[]{:S(2)}, u32[]{:S(2)}) collective-permute-start(f32[8,2]{1,0:T(8,128)S(1)} %convert_element_type.73), channel_id=1, source_target_pairs={{0,6},{1,7},{2,8},{3,9},{4,10},{5,11},{6,12},{7,13},{8,14},{9,15},... | collective-permute-start | bytes 200 | tf_op jit(solution)/shard_map/ppermute | solution.py:17
  75.2 163.7 %collective-permute-start.9 = (f32[8,256,256]{1,2,0:T(8,128)}, f32[8,256,256]{1,2,0:T(8,128)}, u32[]{:S(2)}, u32[]{:S(2)}) collective-permute-start(f32[8,256,256]{1,2,0:T(8,128)} %copy.131), channel_id=1, source_target_pairs={{0,3},{1,4},{2,5},{3,6},{4,7},{5,8},{6,9},{7,10},{8,11},{9,12},{10... | collective-permute-start | bytes 6291464 | tf_op jit(solution)/shard_map/ppermute | solution.py:17
  122.8 119.1 %collective-permute-start.10 = (f32[8,256,256]{1,2,0:T(8,128)}, f32[8,256,256]{1,2,0:T(8,128)}, u32[]{:S(2)}, u32[]{:S(2)}) collective-permute-start(f32[8,256,256]{1,2,0:T(8,128)} %copy.132), channel_id=1, source_target_pairs={{0,4},{1,5},{2,6},{3,7},{4,8},{5,9},{6,10},{7,11},{8,12},{9,13},{1... | collective-permute-start | bytes 6291464 | tf_op jit(solution)/shard_map/ppermute | solution.py:17
  123.2 44.8 %collective-permute-start.6 = (f32[8,2]{1,0:T(8,128)S(1)}, f32[8,2]{1,0:T(8,128)S(1)}, u32[]{:S(2)}, u32[]{:S(2)}) collective-permute-start(f32[8,2]{1,0:T(8,128)S(1)} %convert_element_type.75), channel_id=1, source_target_pairs={{0,7},{1,8},{2,9},{3,10},{4,11},{5,12},{6,13},{7,14},{8,15},{9,0},... | collective-permute-start | bytes 200 | tf_op jit(solution)/shard_map/ppermute | solution.py:17
  167.9 93.1 %collective-permute-start.11 = (f32[8,256,256]{1,2,0:T(8,128)}, f32[8,256,256]{1,2,0:T(8,128)}, u32[]{:S(2)}, u32[]{:S(2)}) collective-permute-start(f32[8,256,256]{1,2,0:T(8,128)} %copy.133), channel_id=1, source_target_pairs={{0,5},{1,6},{2,7},{3,8},{4,9},{5,10},{6,11},{7,12},{8,13},{9,14},{... | collective-permute-start | bytes 6291464 | tf_op jit(solution)/shard_map/ppermute | solution.py:17
  168.4 183.8 %collective-permute-start.12 = (f32[8,256,256]{1,2,0:T(8,128)}, f32[8,256,256]{1,2,0:T(8,128)}, u32[]{:S(2)}, u32[]{:S(2)}) collective-permute-start(f32[8,256,256]{1,2,0:T(8,128)} %copy.134), channel_id=1, source_target_pairs={{0,6},{1,7},{2,8},{3,9},{4,10},{5,11},{6,12},{7,13},{8,14},{9,15},... | collective-permute-start | bytes 6291464 | tf_op jit(solution)/shard_map/ppermute | solution.py:17
  216.0 139.1 %collective-permute-start.13 = (f32[8,256,256]{1,2,0:T(8,128)}, f32[8,256,256]{1,2,0:T(8,128)}, u32[]{:S(2)}, u32[]{:S(2)}) collective-permute-start(f32[8,256,256]{1,2,0:T(8,128)} %copy.135), channel_id=1, source_target_pairs={{0,7},{1,8},{2,9},{3,10},{4,11},{5,12},{6,13},{7,14},{8,15},{9,0},... | collective-permute-start | bytes 6291464 | tf_op jit(solution)/shard_map/ppermute | solution.py:17
  225.3 317.7 %all-to-all-start = ((f32[128,1,2]{2,1,0:T(1,128)}), f32[128,1,2]{2,1,0:T(1,128)S(1)}, u32[]{:S(2)}, u32[]{:S(2)}) async-start(f32[128,1,2]{2,1,0:T(1,128)} %bitcast.10), calls=%async_computation | async-start | bytes 131072 | tf_op jit(solution)/shard_map/all_to_all | solution.py:82
  401.4 3.3 copy-start.3
  542.9 290.0 %all-to-all-start.1 = ((f32[128,2,128,128]{3,2,1,0:T(8,128)}), f32[128,2,128,128]{3,2,1,0:T(8,128)}, u32[]{:S(2)}, u32[]{:S(2)}) async-start(f32[128,2,128,128]{3,2,1,0:T(8,128)} %bitcast.76), calls=%async_computation.1 | async-start | bytes 33554432 | tf_op jit(solution)/shard_map/all_to_all | solution.py:75
  593.5 309.5 %all-gather.3.cloned.1.call-start = ((), (), s32[]{:S(2)}) async-start(), calls=%async_computation.4 | async-start | bytes 1179648 | tf_op jit(solution)/shard_map/all_gather | solution.py:105
  594.2 399.3 %reduce-scatter.3.cloned.1.call-start = ((), (), s32[]{:S(2)}) async-start(), calls=%async_computation.5 | async-start | bytes 2228224 | tf_op jit(solution)/shard_map/reduce_scatter | solution.py:106
  914.6 104.1 %all-gather.5.cloned.1.call-start = ((), (), s32[]{:S(2)}) async-start(), calls=%async_computation.6 | async-start | bytes 1179648 | tf_op jit(solution)/shard_map/all_gather | solution.py:105
  914.7 78.8 %copy-start.7 = (f32[128,256]{1,0:T(8,128)S(1)}, f32[128,256]{1,0:T(8,128)}, u32[]{:S(2)}) copy-start(f32[128,256]{1,0:T(8,128)} %param.18) | copy-start | bytes 393220
  914.7 78.8 %copy-start.8 = (f32[128,256]{1,0:T(8,128)S(1)}, f32[128,256]{1,0:T(8,128)}, u32[]{:S(2)}) copy-start(f32[128,256]{1,0:T(8,128)} %param.19) | copy-start | bytes 393220
  995.2 110.1 %reduce-scatter.5.cloned.1.call-start = ((), (), s32[]{:S(2)}) async-start(), calls=%async_computation.7 | async-start | bytes 2228224 | tf_op jit(solution)/shard_map/reduce_scatter | solution.py:106
  1018.7 88.3 %copy-start.1 = (f32[16,256]{1,0:T(8,128)S(1)}, f32[16,256]{1,0:T(8,128)}, u32[]{:S(2)}) copy-start(f32[16,256]{1,0:T(8,128)} %param.17) | copy-start | bytes 49156
  1030.2 75.2 %copy-start.6 = (f32[128,256]{1,0:T(8,128)S(1)}, f32[128,256]{1,0:T(8,128)}, u32[]{:S(2)}) copy-start(f32[128,256]{1,0:T(8,128)} %divide_add_fusion.1) | copy-start | bytes 393220
Sparse Core Ops, SparseCore 0:
  596.0 93.5 all-gather.2
  914.7 78.7 reduce-scatter.2
  995.8 22.8 all-gather.4
  1030.3 74.9 reduce-scatter.4
where the time goes:
time: 1120 us; the launch traced here: 1110 us
  waiting for transfers between devices  558 us (50%)
  starting transfers between devices  176 us (16%)
  local copies, waits for them, and re-layouts  164 us (15%)
  other arithmetic  114 us (10%)
  matrix products  87.9 us (8%)
  between operations  14.3 us (1%)
    all_to_all x1, waiting for transfers between devices, on_device(): lax.all_to_all(sent_blocks.reshape(dev_count, slot_cap, CB, CB), ('row',...  238 us
    ppermute x14, waiting for transfers between devices, from_behind(): return lax.ppermute(value, axis, pairs)  148 us
    reduce_scatter x2, waiting for transfers between devices, on_device(): lax.psum_scatter(jnp.dot(matrix, gathered, precision=highest), 'col', sca...  147 us
    ppermute x14, starting transfers between devices, from_behind(): return lax.ppermute(value, axis, pairs)  117 us
    scatter-add x1, other arithmetic, on_device(): jax.ops.segment_sum(got_blocks.reshape(-1, CB, CB), places, num_segments=...  51.8 us
    scatter-add x1, other arithmetic, on_device(): jax.ops.segment_sum(partial_value, slot, num_segments=dev_count * slot_ca...  51.5 us
    all_to_all x1, starting transfers between devices, on_device(): lax.all_to_all(sent_blocks.reshape(dev_count, slot_cap, CB, CB), ('row',...  50.5 us
    reshape x2, local copies, waits for them, and re-layouts, on_device(): partial_value.reshape(local_rows, KA, KP, CB, KP, CB)  45.7 us
  transfers between devices with their start and end apart: 20, of which 7 were waited for; matrix products, arithmetic and copies ran while one was open for 30% of the time, Pallas kernels for 0%

commit v1 on v0

--- a/solution.py
+++ b/solution.py
@@ -102,7 +102,9 @@
     floor_diag = jnp.maximum(jnp.abs(jnp.diagonal(own_block)), 1.0)
     current = guess
     for sweep in range(2):
-        gathered = lax.all_gather(current, "row", axis=0, tiled=True)
+        gathered = jnp.concatenate(
+            lax.all_to_all(jnp.stack([current] * lax.axis_size("row")), "row", 0, 0), axis=0
+        )
         applied = lax.psum_scatter(
             jnp.dot(matrix, gathered, precision=highest), "col", scatter_dimension=0, tiled=True
         )

time: 1120 us -> 1070 us (0.955)
  waiting for transfers between devices: 558 us -> 288 us
  blocking collectives: 0 us -> 257 us
  starting transfers between devices: 176 us -> 129 us
    all_to_all x0 -> x2, blocking collectives: none -> 257 us  [the longest x1 237 us: on_device(): lax.all_to_all(sent_blocks.reshape(dev_count, slot_cap, CB, CB), ('row',...]
    all_to_all x1, waiting for transfers between devices: 238 us -> 0.01 us  [on_device(): lax.all_to_all(jnp.stack([current] * lax.axis_size('row')), 'row', 0, 0)]
    all_to_all x1, starting transfers between devices: 50.5 us -> 3.56 us  [on_device(): lax.all_to_all(jnp.stack([current] * lax.axis_size('row')), 'row', 0, 0)]
    all_gather x2 -> x0, waiting for transfers between devices: 23.5 us -> none  [on_device(): gathered = lax.all_gather(current, 'row', axis=0, tiled=True)]
    unnamed x41 -> x39, local copies, waits for them, and re-layouts: 30 us -> 30.1 us
  transfers between devices with their start and end apart: 20 -> 18, of which waited for: 7 -> 5; matrix products, arithmetic and copies ran while one was open for 30% -> 32% of each run, Pallas kernels for 0% -> 0%
where the time goes in v1:
time: 1070 us; the launch traced here: 1060 us
  waiting for transfers between devices  288 us (27%)
  blocking collectives  257 us (24%)
  local copies, waits for them, and re-layouts  165 us (15%)
  starting transfers between devices  129 us (12%)
  other arithmetic  114 us (11%)
  matrix products  87.3 us (8%)
  between operations  14.6 us (1%)
    all_to_all x1, blocking collectives, on_device(): lax.all_to_all(sent_blocks.reshape(dev_count, slot_cap, CB, CB), ('row',...  237 us
    ppermute x14, waiting for transfers between devices, from_behind(): return lax.ppermute(value, axis, pairs)  148 us
    reduce_scatter x2, waiting for transfers between devices, on_device(): lax.psum_scatter(jnp.dot(matrix, gathered, precision=highest), 'col', sca...  140 us
    ppermute x14, starting transfers between devices, from_behind(): return lax.ppermute(value, axis, pairs)  117 us
    scatter-add x1, other arithmetic, on_device(): jax.ops.segment_sum(got_blocks.reshape(-1, CB, CB), places, num_segments=...  52 us
    scatter-add x1, other arithmetic, on_device(): jax.ops.segment_sum(partial_value, slot, num_segments=dev_count * slot_ca...  51.5 us
    reshape x2, local copies, waits for them, and re-layouts, on_device(): partial_value.reshape(local_rows, KA, KP, CB, KP, CB)  45.7 us
    dot_general x1, matrix products, on_device(): jnp.einsum('skab,skbn->skan', a_blocks, ghost_p, precision=highest)  43.2 us
  transfers between devices with their start and end apart: 18, of which 5 were waited for; matrix products, arithmetic and copies ran while one was open for 32% of the time, Pallas kernels for 0%

profile of v1, /device:TPU:0, one launch (start us, length us, event | category | flops | bytes accessed | tf_op | source)
XLA Modules:
  0.0 1055.1 jit_solution(14870073482332205015)
XLA Ops:
  9.8 3.4 collective-permute-start.1
  15.0 3.6 collective-permute-start.2
  34.1 4.1 copy.128
  50.5 4.1 reshape.502
  56.5 3.1 copy.132
  75.2 47.5 %collective-permute-start.9 = (f32[8,256,256]{1,2,0:T(8,128)}, f32[8,256,256]{1,2,0:T(8,128)}, u32[]{:S(2)}, u32[]{:S(2)}) collective-permute-start(f32[8,256,256]{1,2,0:T(8,128)} %copy.131), channel_id=1, source_target_pairs={{0,3},{1,4},{2,5},{3,6},{4,7},{5,8},{6,9},{7,10},{8,11},{9,12},{10... | collective-permute-start | bytes 6291464 | tf_op jit(solution)/shard_map/ppermute | solution.py:17
  123.9 44.1 %collective-permute-done.6 = f32[8,2]{1,0:T(8,128)S(1)} collective-permute-done((f32[8,2]{1,0:T(8,128)S(1)}, f32[8,2]{1,0:T(8,128)S(1)}, u32[]{:S(2)}, u32[]{:S(2)}) %collective-permute-start.6) | collective-permute-done | bytes 96 | tf_op jit(solution)/shard_map/ppermute | solution.py:17
  168.4 47.2 %collective-permute-start.12 = (f32[8,256,256]{1,2,0:T(8,128)}, f32[8,256,256]{1,2,0:T(8,128)}, u32[]{:S(2)}, u32[]{:S(2)}) collective-permute-start(f32[8,256,256]{1,2,0:T(8,128)} %copy.134), channel_id=1, source_target_pairs={{0,6},{1,7},{2,8},{3,9},{4,10},{5,11},{6,12},{7,13},{8,14},{9,15},... | collective-permute-start | bytes 6291464 | tf_op jit(solution)/shard_map/ppermute | solution.py:17
  216.0 6.1 collective-permute-start.13
  225.3 7.6 all-to-all-start
  245.0 16.1 %collective-permute-done.11 = f32[8,256,256]{1,2,0:T(8,128)} collective-permute-done((f32[8,256,256]{1,2,0:T(8,128)}, f32[8,256,256]{1,2,0:T(8,128)}, u32[]{:S(2)}, u32[]{:S(2)}) %collective-permute-start.11) | collective-permute-done | bytes 2097184 | tf_op jit(solution)/shard_map/ppermute | solution.py:17
  264.1 88.1 %collective-permute-done.12 = f32[8,256,256]{1,2,0:T(8,128)} collective-permute-done((f32[8,256,256]{1,2,0:T(8,128)}, f32[8,256,256]{1,2,0:T(8,128)}, u32[]{:S(2)}, u32[]{:S(2)}) %collective-permute-start.12) | collective-permute-done | bytes 2097184 | tf_op jit(solution)/shard_map/ppermute | solution.py:17
  358.2 43.2 %multiply_bitcast_fusion = f32[8,8,256,256]{2,3,1,0:T(8,128)} fusion(f32[8,8,256,256]{2,3,1,0:T(8,128)} %bitcast_dynamic-update-slice_fusion, f32[8,8,256,256]{3,2,1,0:T(8,128)} %param.11, f32[8,8]{1,0:T(8,128)S(1)} %convert_element_type.80), kind=kOutput, calls=%fused_computation.18 | convolution fusion | flops 12889096192 | bytes 50331904 | tf_op jit(solution)/shard_map/skab,skbn->skan/dot_general | solution.py:46
  401.4 3.3 fusion
  404.7 21.4 %convolution_bitcast_fusion = f32[8,8,256,256]{2,3,1,0:T(8,128)} fusion(f32[8,8,256,256]{2,3,1,0:T(8,128)} %fusion, f32[8,256,256,1]{2,1,0,3:T(8,128)S(1)} %copy-done.3), kind=kOutput, calls=%fused_computation.19 | convolution fusion | flops 12884901888 | bytes 35651584 | tf_op jit(solution)/shard_map/sam,skan->skmn/dot_general | solution.py:49
  426.1 20.8 %reshape.352 = f32[8,8,2,128,2,128]{3,2,5,4,1,0:T(2,128)} reshape(f32[8,8,256,256]{2,3,1,0:T(8,128)} %convolution_bitcast_fusion) | data formatting | bytes 33554432 | tf_op jit(solution)/shard_map/reshape | solution.py:51
  446.9 25.0 %copy.136 = f32[8,8,2,128,2,128]{5,3,4,2,1,0:T(8,128)} copy(f32[8,8,2,128,2,128]{3,2,5,4,1,0:T(2,128)} %reshape.352) | data formatting | bytes 33554432 | tf_op jit(solution)/shard_map/reshape | solution.py:51
  471.8 7.9 broadcast_in_dim.27
  479.7 51.5 %scatter_fusion = f32[257,128,128]{2,1,0:T(8,128)} fusion(f32[257,128,128]{2,1,0:T(8,128)} %broadcast_in_dim.27, s32[256]{0:T(256)S(1)} %bitcast.88, f32[256,128,128]{2,1,0:T(8,128)} %bitcast.80), kind=kCustom, calls=%fused_computation.16 | custom fusion | flops 4194304 | bytes 50332672 | tf_op jit(solution)/shard_map/scatter-add | solution.py:68
  531.2 11.6 %slice.99 = f32[256,128,128]{2,1,0:T(8,128)} slice(f32[257,128,128]{2,1,0:T(8,128)} %scatter_fusion), slice={[0:256], [0:128], [0:128]} | slice | bytes 33554432 | tf_op jit(solution)/shard_map/slice | solution.py:68
  542.9 237.0 %all_to_all.24 = f32[128,2,128,128]{3,2,1,0:T(8,128)} all-to-all(f32[128,2,128,128]{3,2,1,0:T(8,128)} %bitcast.79), channel_id=1, replica_groups=mesh['row'=8,'col'=16] {'row','col'}, dimensions={0} | all-to-all | bytes 33554432 | tf_op jit(solution)/shard_map/all_to_all | solution.py:75
  781.0 3.6 all-to-all-start.2
  785.3 4.3 broadcast_in_dim.20
  789.6 52.0 %scatter_fusion.1 = f32[129,128,128]{2,1,0:T(8,128)} fusion(f32[129,128,128]{2,1,0:T(8,128)} %broadcast_in_dim.20, s32[256]{0:T(256)S(1)} %bitcast.89, f32[256,128,128]{2,1,0:T(8,128)} %bitcast.78), kind=kCustom, calls=%fused_computation.17 | custom fusion | flops 4194304 | bytes 50332672 | tf_op jit(solution)/shard_map/scatter-add | solution.py:92
  841.7 4.0 slice.100
  845.7 9.9 copy.137
  855.6 11.3 %fusion.20 = f32[2048,256]{1,0:T(8,128)} fusion(f32[1024,256]{1,0:T(8,128)S(1)} %bitcast.85, f32[256,8,8,128]{3,2,1,0:T(8,128)} %bitcast.74), kind=kOutput, calls=%fused_computation.105 | convolution fusion | flops 6442450944 | bytes 11534336 | tf_op jit(solution)/shard_map/dot_general | solution.py:109
  867.0 5.5 copy.145
  873.8 67.4 %reduce-scatter.3.cloned.1.call-done = f32[128,256]{1,0:T(8,128)} async-done(((f32[2048,256]{1,0:T(8,128)}), f32[128,256]{1,0:T(8,128)}) %reduce-scatter.3.cloned.1.call-update) | async-done | bytes 131088 | tf_op jit(solution)/shard_map/reduce_scatter | solution.py:108
  942.3 20.2 %all_to_all.25 = f32[8,128,256]{2,1,0:T(8,128)S(1)} all-to-all(f32[8,128,256]{2,1,0:T(8,128)S(1)} %stack.91), channel_id=1, replica_groups=mesh['row'=8,'col'=16] {'row'}, dimensions={0} | all-to-all | bytes 2097152 | tf_op jit(solution)/shard_map/all_to_all | solution.py:106
  962.5 11.2 %fusion.19 = f32[2048,256]{1,0:T(8,128)} fusion(f32[1024,256]{1,0:T(8,128)S(1)} %bitcast.86, f32[256,8,8,128]{3,2,1,0:T(8,128)} %bitcast.76), kind=kOutput, calls=%fused_computation.104 | convolution fusion | flops 6442450944 | bytes 11534336 | tf_op jit(solution)/shard_map/dot_general | solution.py:109
  973.8 72.6 %reduce-scatter.5.cloned.1.call-done = f32[128,256]{1,0:T(8,128)} async-done(((f32[2048,256]{1,0:T(8,128)}), f32[128,256]{1,0:T(8,128)}) %reduce-scatter.5.cloned.1.call-update) | async-done | bytes 131088 | tf_op jit(solution)/shard_map/reduce_scatter | solution.py:108
  (142 shorter events, 81.9 us)
Async XLA Ops:
  7.2 25.8 %copy-start = (f32[16,256]{1,0:T(8,128)S(1)}, f32[16,256]{1,0:T(8,128)}, u32[]{:S(2)}) copy-start(f32[16,256]{1,0:T(8,128)} %param.17) | copy-start | bytes 49156
  9.8 59.1 %collective-permute-start.1 = (f32[8,2]{1,0:T(8,128)S(1)}, f32[8,2]{1,0:T(8,128)S(1)}, u32[]{:S(2)}, u32[]{:S(2)}) collective-permute-start(f32[8,2]{1,0:T(8,128)S(1)} %convert_element_type.65), channel_id=1, source_target_pairs={{0,2},{1,3},{2,4},{3,5},{4,6},{5,7},{6,8},{7,9},{8,10},{9,11},{10,... | collective-permute-start | bytes 200 | tf_op jit(solution)/shard_map/ppermute | solution.py:17
  13.7 56.5 %collective-permute-start = (f32[8,2]{1,0:T(8,128)S(1)}, f32[8,2]{1,0:T(8,128)S(1)}, u32[]{:S(2)}, u32[]{:S(2)}) collective-permute-start(f32[8,2]{1,0:T(8,128)S(1)} %convert_element_type.63), channel_id=1, source_target_pairs={{0,1},{1,2},{2,3},{3,4},{4,5},{5,6},{6,7},{7,8},{8,9},{9,10},{10,1... | collective-permute-start | bytes 200 | tf_op jit(solution)/shard_map/ppermute | solution.py:17
  15.0 57.9 %collective-permute-start.2 = (f32[8,2]{1,0:T(8,128)S(1)}, f32[8,2]{1,0:T(8,128)S(1)}, u32[]{:S(2)}, u32[]{:S(2)}) collective-permute-start(f32[8,2]{1,0:T(8,128)S(1)} %convert_element_type.67), channel_id=1, source_target_pairs={{0,3},{1,4},{2,5},{3,6},{4,7},{5,8},{6,9},{7,10},{8,11},{9,12},{10... | collective-permute-start | bytes 200 | tf_op jit(solution)/shard_map/ppermute | solution.py:17
  26.4 142.0 %collective-permute-start.8 = (f32[8,256,256]{1,2,0:T(8,128)}, f32[8,256,256]{1,2,0:T(8,128)}, u32[]{:S(2)}, u32[]{:S(2)}) collective-permute-start(f32[8,256,256]{1,2,0:T(8,128)} %copy.130), channel_id=1, source_target_pairs={{0,2},{1,3},{2,4},{3,5},{4,6},{5,7},{6,8},{7,9},{8,10},{9,11},{10,... | collective-permute-start | bytes 6291464 | tf_op jit(solution)/shard_map/ppermute | solution.py:17
  28.5 4.5 copy-start.9
  28.5 4.5 copy-start.8
  28.5 4.5 copy-start.10
  31.4 184.6 %collective-permute-start.7 = (f32[8,256,256]{1,2,0:T(8,128)}, f32[8,256,256]{1,2,0:T(8,128)}, u32[]{:S(2)}, u32[]{:S(2)}) collective-permute-start(f32[8,256,256]{1,2,0:T(8,128)} %copy.129), channel_id=1, source_target_pairs={{0,1},{1,2},{2,3},{3,4},{4,5},{5,6},{6,7},{7,8},{8,9},{9,10},{10,1... | collective-permute-start | bytes 6291464 | tf_op jit(solution)/shard_map/ppermute | solution.py:17
  50.5 4.1 copy-start.4
  56.5 3.1 copy-start.5
  61.4 3.0 copy-start.2
  68.9 6.4 collective-permute-start.3
  70.2 52.7 %collective-permute-start.4 = (f32[8,2]{1,0:T(8,128)S(1)}, f32[8,2]{1,0:T(8,128)S(1)}, u32[]{:S(2)}, u32[]{:S(2)}) collective-permute-start(f32[8,2]{1,0:T(8,128)S(1)} %convert_element_type.71), channel_id=1, source_target_pairs={{0,5},{1,6},{2,7},{3,8},{4,9},{5,10},{6,11},{7,12},{8,13},{9,14},{... | collective-permute-start | bytes 200 | tf_op jit(solution)/shard_map/ppermute | solution.py:17
  73.0 50.2 %collective-permute-start.5 = (f32[8,2]{1,0:T(8,128)S(1)}, f32[8,2]{1,0:T(8,128)S(1)}, u32[]{:S(2)}, u32[]{:S(2)}) collective-permute-start(f32[8,2]{1,0:T(8,128)S(1)} %convert_element_type.73), channel_id=1, source_target_pairs={{0,6},{1,7},{2,8},{3,9},{4,10},{5,11},{6,12},{7,13},{8,14},{9,15},... | collective-permute-start | bytes 200 | tf_op jit(solution)/shard_map/ppermute | solution.py:17
  75.2 163.7 %collective-permute-start.9 = (f32[8,256,256]{1,2,0:T(8,128)}, f32[8,256,256]{1,2,0:T(8,128)}, u32[]{:S(2)}, u32[]{:S(2)}) collective-permute-start(f32[8,256,256]{1,2,0:T(8,128)} %copy.131), channel_id=1, source_target_pairs={{0,3},{1,4},{2,5},{3,6},{4,7},{5,8},{6,9},{7,10},{8,11},{9,12},{10... | collective-permute-start | bytes 6291464 | tf_op jit(solution)/shard_map/ppermute | solution.py:17
  122.9 119.1 %collective-permute-start.10 = (f32[8,256,256]{1,2,0:T(8,128)}, f32[8,256,256]{1,2,0:T(8,128)}, u32[]{:S(2)}, u32[]{:S(2)}) collective-permute-start(f32[8,256,256]{1,2,0:T(8,128)} %copy.132), channel_id=1, source_target_pairs={{0,4},{1,5},{2,6},{3,7},{4,8},{5,9},{6,10},{7,11},{8,12},{9,13},{1... | collective-permute-start | bytes 6291464 | tf_op jit(solution)/shard_map/ppermute | solution.py:17
  123.2 44.8 %collective-permute-start.6 = (f32[8,2]{1,0:T(8,128)S(1)}, f32[8,2]{1,0:T(8,128)S(1)}, u32[]{:S(2)}, u32[]{:S(2)}) collective-permute-start(f32[8,2]{1,0:T(8,128)S(1)} %convert_element_type.75), channel_id=1, source_target_pairs={{0,7},{1,8},{2,9},{3,10},{4,11},{5,12},{6,13},{7,14},{8,15},{9,0},... | collective-permute-start | bytes 200 | tf_op jit(solution)/shard_map/ppermute | solution.py:17
  168.0 93.1 %collective-permute-start.11 = (f32[8,256,256]{1,2,0:T(8,128)}, f32[8,256,256]{1,2,0:T(8,128)}, u32[]{:S(2)}, u32[]{:S(2)}) collective-permute-start(f32[8,256,256]{1,2,0:T(8,128)} %copy.133), channel_id=1, source_target_pairs={{0,5},{1,6},{2,7},{3,8},{4,9},{5,10},{6,11},{7,12},{8,13},{9,14},{... | collective-permute-start | bytes 6291464 | tf_op jit(solution)/shard_map/ppermute | solution.py:17
  168.4 183.7 %collective-permute-start.12 = (f32[8,256,256]{1,2,0:T(8,128)}, f32[8,256,256]{1,2,0:T(8,128)}, u32[]{:S(2)}, u32[]{:S(2)}) collective-permute-start(f32[8,256,256]{1,2,0:T(8,128)} %copy.134), channel_id=1, source_target_pairs={{0,6},{1,7},{2,8},{3,9},{4,10},{5,11},{6,12},{7,13},{8,14},{9,15},... | collective-permute-start | bytes 6291464 | tf_op jit(solution)/shard_map/ppermute | solution.py:17
  216.0 139.2 %collective-permute-start.13 = (f32[8,256,256]{1,2,0:T(8,128)}, f32[8,256,256]{1,2,0:T(8,128)}, u32[]{:S(2)}, u32[]{:S(2)}) collective-permute-start(f32[8,256,256]{1,2,0:T(8,128)} %copy.135), channel_id=1, source_target_pairs={{0,7},{1,8},{2,9},{3,10},{4,11},{5,12},{6,13},{7,14},{8,15},{9,0},... | collective-permute-start | bytes 6291464 | tf_op jit(solution)/shard_map/ppermute | solution.py:17
  225.3 317.6 %all-to-all-start = ((f32[128,1,2]{2,1,0:T(1,128)}), f32[128,1,2]{2,1,0:T(1,128)S(1)}, u32[]{:S(2)}, u32[]{:S(2)}) async-start(f32[128,1,2]{2,1,0:T(1,128)} %bitcast.10), calls=%async_computation | async-start | bytes 131072 | tf_op jit(solution)/shard_map/all_to_all | solution.py:82
  401.4 3.3 copy-start.3
  542.9 237.0 %copy-start.6 = (f32[128,256]{1,0:T(8,128)S(1)}, f32[128,256]{1,0:T(8,128)}, u32[]{:S(2)}) copy-start(f32[128,256]{1,0:T(8,128)} %param.19) | copy-start | bytes 393220
  781.0 74.6 %all-to-all-start.2 = ((f32[8,128,256]{2,1,0:T(8,128)}), f32[8,128,256]{2,1,0:T(8,128)S(1)}, u32[]{:S(2)}, u32[]{:S(2)}) async-start(f32[8,128,256]{2,1,0:T(8,128)} %stack.90), calls=%async_computation.2 | async-start | bytes 2097152 | tf_op jit(solution)/shard_map/all_to_all | solution.py:106
  784.5 156.7 %reduce-scatter.3.cloned.1.call-start = ((), (), s32[]{:S(2)}) async-start(), calls=%async_computation.6 | async-start | bytes 2228224 | tf_op jit(solution)/shard_map/reduce_scatter | solution.py:108
  867.0 179.4 %reduce-scatter.5.cloned.1.call-start = ((), (), s32[]{:S(2)}) async-start(), calls=%async_computation.7 | async-start | bytes 2228224 | tf_op jit(solution)/shard_map/reduce_scatter | solution.py:108
  867.0 74.2 %copy-start.7 = (f32[128,256]{1,0:T(8,128)S(1)}, f32[128,256]{1,0:T(8,128)}, u32[]{:S(2)}) copy-start(f32[128,256]{1,0:T(8,128)} %param.18) | copy-start | bytes 393220
  962.5 85.5 %copy-start.1 = (f32[16,256]{1,0:T(8,128)S(1)}, f32[16,256]{1,0:T(8,128)}, u32[]{:S(2)}) copy-start(f32[16,256]{1,0:T(8,128)} %param.17) | copy-start | bytes 49156
Sparse Core Ops, SparseCore 0:
  867.1 74.1 reduce-scatter.2
  973.9 72.4 reduce-scatter.4
